TPU v7x, 32 devices: a whole 2x2x4 slice. The times are simulated.
32 devices in a mesh: groups: 2 (over y), markov: 4 (over z), storage: 2 (over x), sub: 2 (over core).
Axes of the slice: x: 2, y: 2, z: 4, core: 2. Of those that a mesh axis runs over, the one named last changes fastest.
Arguments:
- expected_cot: bfloat16 [8192, 2048], P(('groups', 'markov'), ('storage', 'sub')), parts along dimension 0, may hold values from -192 to 192
- value_next: bfloat16 [8192, 2048], P(('groups', 'markov'), ('storage', 'sub')), parts along dimension 0, may hold values from -0.0024414062 to 0.0024414062
- transition: bfloat16 [8192, 4096], P(('groups', 'storage', 'sub'), 'markov'), parts along dimension 0, may hold values from 6.1035156e-05 to 0.0009765625
- section: int32 [2], P('groups'), parts along dimension 0, may hold values from 0 to 51
Outputs:
- section_adjoint: float32 [8192, 2048], P(('groups', 'markov'), ('storage', 'sub')), parts along dimension 0
- transition_grad: float32 [8192, 4096], P(('groups', 'storage', 'sub'), 'markov'), parts along dimension 0
There are 2 independent parts, one for each index of `groups`. A program takes and returns all parts, laid end to end along the dimension named above; each array names one. Nothing has to cross between parts.
All inputs are finite; a program needn't handle non-finite values.
Results may differ from a plain program's by a relative error of at most 0.0003.
Values may be sent and summed in bfloat16 or wider, within the bound.
A program may use at most 64 MiB of HBM per device.

v0:
```python
import jax
import jax.numpy as jnp
from jax import lax
from jax.sharding import PartitionSpec as P

discount_rate = 0.97


def shards(expected_cot, value_next, transition, section):
    discount_factor = jnp.exp(section[0].astype(jnp.float32) * jnp.log(jnp.float32(discount_rate)))
    cotangent_all = lax.all_gather(expected_cot, "markov", axis=0, tiled=True)
    adjoint_sum = lax.dot_general(
        lax.all_gather(transition, ("storage", "sub"), axis=0, tiled=True),
        cotangent_all,
        (((0,), (0,)), ((), ())),
        preferred_element_type=jnp.float32,
    )
    own_states = lax.all_to_all(
        cotangent_all, ("storage", "sub"), split_axis=0, concat_axis=1, tiled=True
    )
    gathered_values = lax.all_gather(value_next, ("storage", "sub"), axis=1, tiled=True)
    gradient_sum = lax.dot_general(
        own_states, gathered_values, (((1,), (1,)), ((), ())), preferred_element_type=jnp.float32
    )
    return (discount_factor * adjoint_sum, discount_factor * gradient_sum)


def solution(mesh):
    return jax.shard_map(
        shards,
        mesh=mesh,
        in_specs=(
            P(("groups", "markov"), ("storage", "sub")),
            P(("groups", "markov"), ("storage", "sub")),
            P(("groups", "storage", "sub"), "markov"),
            P("groups"),
        ),
        out_specs=(
            P(("groups", "markov"), ("storage", "sub")),
            P(("groups", "storage", "sub"), "markov"),
        ),
        check_vma=False,
    )
```

profile of v0, /device:TPU:0, one launch (start us, length us, event | category | flops | bytes accessed | tf_op | source)
XLA Modules:
  0.0 232.1 jit_solution(16197326605313307399)
XLA Ops:
  7.2 0.0 all-gather.6.cloned.1.call-start
  7.2 0.7 all-gather.6.cloned.1.call-update
  7.9 0.0 all-gather.8.cloned.1.call-start
  7.9 0.7 all-gather.8.cloned.1.call-update
  8.6 0.0 all-gather.4.cloned.1.call-start
  8.7 0.7 all-gather.4.cloned.1.call-update
  9.4 83.7 %all-gather.6.cloned.1.call-done = bf16[4096,512]{1,0:T(8,128)(2,1)} async-done(((bf16[1024,512]{1,0:T(8,128)(2,1)}), bf16[4096,512]{1,0:T(8,128)(2,1)}) %all-gather.6.cloned.1.call-update) | async-done | bytes 4194320 | tf_op jit(solution)/shard_map/all_gather | solution.py:11
  93.0 4.9 %all-to-all-start = ((bf16[4,1024,512]{2,1,0:T(8,128)(2,1)}), bf16[4,1024,512]{2,1,0:T(8,128)(2,1)}, u32[]{:S(2)}, u32[]{:S(2)}) async-start(bf16[4,1024,512]{2,1,0:T(8,128)(2,1)} %bitcast.8), calls=%async_computation | async-start | bytes 8388608 | tf_op jit(solution)/shard_map/all_to_all | solution.py:18
  98.6 75.7 %all-to-all-done = bf16[4,1024,512]{2,1,0:T(8,128)(2,1)} async-done(((bf16[4,1024,512]{2,1,0:T(8,128)(2,1)}), bf16[4,1024,512]{2,1,0:T(8,128)(2,1)}, u32[]{:S(2)}, u32[]{:S(2)}) %all-to-all-start) | async-done | bytes 4194336 | tf_op jit(solution)/shard_map/all_to_all | solution.py:18
  174.3 6.3 %copy.6 = bf16[1024,4,512]{0,2,1:T(8,128)(2,1)} copy(bf16[1024,4,512]{2,0,1:T(8,128)(2,1)} %bitcast.2) | data formatting | bytes 8388608 | tf_op jit(solution)/shard_map/all_to_all | solution.py:18
  180.6 0.0 all-gather.8.cloned.1.call-done
  180.6 10.0 %convolution_multiply_fusion = f32[1024,1024]{1,0:T(8,128)} fusion(bf16[1024,2048]{0,1:T(8,128)(2,1)} %bitcast.9, bf16[1024,2048]{1,0:T(8,128)(2,1)} %all-gather.8.cloned.1.call-done, f32[]{:T(128)} %bitcast), kind=kOutput, calls=%fused_computation | convolution fusion | flops 4296015872 | bytes 12582916 | tf_op jit(solution)/shard_map/dot_general | solution.py:22
  190.6 24.5 %all-gather.4.cloned.1.call-done = bf16[4096,1024]{1,0:T(8,128)(2,1)} async-done(((bf16[1024,1024]{1,0:T(8,128)(2,1)}), bf16[4096,1024]{1,0:T(8,128)(2,1)}) %all-gather.4.cloned.1.call-update) | async-done | bytes 8388624 | tf_op jit(solution)/shard_map/all_gather | solution.py:13
  215.2 10.4 %convolution_multiply_fusion.1 = f32[1024,512]{1,0:T(8,128)} fusion(bf16[4096,1024]{1,0:T(8,128)(2,1)} %all-gather.4.cloned.1.call-done, bf16[4096,512]{1,0:T(8,128)(2,1)} %all-gather.6.cloned.1.call-done, f32[]{:T(128)} %bitcast), kind=kOutput, calls=%fused_computation.1 | convolution fusion | flops 4295491584 | bytes 14680068 | tf_op jit(solution)/shard_map/dot_general | solution.py:12
Async XLA Ops:
  7.2 85.9 %all-gather.6.cloned.1.call-start = ((), (), s32[]{:S(2)}) async-start(), calls=%async_computation.2 | async-start | bytes 5242880 | tf_op jit(solution)/shard_map/all_gather | solution.py:11
  7.9 172.7 %all-gather.8.cloned.1.call-start = ((), (), s32[]{:S(2)}) async-start(), calls=%async_computation.3 | async-start | bytes 5242880 | tf_op jit(solution)/shard_map/all_gather | solution.py:21
  8.6 206.5 %all-gather.4.cloned.1.call-start = ((), (), s32[]{:S(2)}) async-start(), calls=%async_computation.1 | async-start | bytes 10485760 | tf_op jit(solution)/shard_map/all_gather | solution.py:13
  93.0 81.2 %all-to-all-start = ((bf16[4,1024,512]{2,1,0:T(8,128)(2,1)}), bf16[4,1024,512]{2,1,0:T(8,128)(2,1)}, u32[]{:S(2)}, u32[]{:S(2)}) async-start(bf16[4,1024,512]{2,1,0:T(8,128)(2,1)} %bitcast.8), calls=%async_computation | async-start | bytes 8388608 | tf_op jit(solution)/shard_map/all_to_all | solution.py:18
Sparse Core Ops, SparseCore 0:
  9.5 83.4 all-gather.5
  94.6 55.5 all-gather.7
  151.7 63.4 all-gather.3
where the time goes:
time: 232 us
  waiting for transfers between devices  186 us (80%)
  matrix products  20.4 us (9%)
  between operations  14.4 us (6%)
  local copies, waits for them, and re-layouts  6.35 us (3%)
  starting transfers between devices  4.97 us (2%)
    all_gather x1, waiting for transfers between devices, shards(): cotangent_all = lax.all_gather(expected_cot, 'markov', axis=0, tiled=True)  83.7 us
    all_to_all x1, waiting for transfers between devices, shards(): lax.all_to_all(cotangent_all, ('storage', 'sub'), split_axis=0, concat_ax...  75.7 us
    all_gather x1, waiting for transfers between devices, shards(): lax.all_gather(transition, ('storage', 'sub'), axis=0, tiled=True)  24.5 us
    dot_general x1, matrix products, shards(): lax.dot_general(lax.all_gather(transition, ('storage', 'sub'), axis=0, ti...  10.4 us
    dot_general x1, matrix products, shards(): lax.dot_general(own_states, gathered_values, (((1,), (1,)), ((), ())), pr...  10 us
    all_to_all x1, local copies, waits for them, and re-layouts, shards(): lax.all_to_all(cotangent_all, ('storage', 'sub'), split_axis=0, concat_ax...  6.35 us
    all_to_all x1, starting transfers between devices, shards(): lax.all_to_all(cotangent_all, ('storage', 'sub'), split_axis=0, concat_ax...  4.85 us
  transfers between devices with their start and end apart: 4, of which 3 were waited for; matrix products, arithmetic and copies ran while one was open for 7% of the time, Pallas kernels for 0%

commit v1 on v0

--- a/solution.py
+++ b/solution.py
@@ -8,7 +8,31 @@
 
 def shards(expected_cot, value_next, transition, section):
     discount_factor = jnp.exp(section[0].astype(jnp.float32) * jnp.log(jnp.float32(discount_rate)))
-    cotangent_all = lax.all_gather(expected_cot, "markov", axis=0, tiled=True)
+    front = jax.lax.axis_size("markov")
+    mixed_arr = jax.lax.axis_index("markov")
+    outer, f_now, w1 = (front, mixed_arr, expected_cot.shape[0])
+    queue = []
+    for at, tick in enumerate(expected_cot.shape):
+        queue.append(tick * outer if at == 0 else tick)
+    e_now = jnp.zeros(queue, expected_cot.dtype)
+    cotangent_all = lax.dynamic_update_slice_in_dim(e_now, expected_cot, f_now * w1, axis=0)
+    x_next = q_next = expected_cot
+    for k0 in range(1, outer // 2 + 1):
+        arrivals = []
+        for at in range(outer):
+            arrivals.append((at, (at + 1) % outer))
+        x_next = jax.lax.ppermute(x_next, "markov", arrivals)
+        cotangent_all = lax.dynamic_update_slice_in_dim(
+            cotangent_all, x_next, (f_now - k0) % outer * w1, axis=0
+        )
+        if 2 * k0 < outer:
+            bank = []
+            for at in range(outer):
+                bank.append((at, (at - 1) % outer))
+            q_next = jax.lax.ppermute(q_next, "markov", bank)
+            cotangent_all = lax.dynamic_update_slice_in_dim(
+                cotangent_all, q_next, (f_now + k0) % outer * w1, axis=0
+            )
     adjoint_sum = lax.dot_general(
         lax.all_gather(transition, ("storage", "sub"), axis=0, tiled=True),
         cotangent_all,

time: 232 us -> 183 us (0.79)
  waiting for transfers between devices: 186 us -> 128 us
  local copies, waits for them, and re-layouts: 6.35 us -> 12.1 us
  starting transfers between devices: 4.97 us -> 10.1 us
    all_gather x1 -> x0, waiting for transfers between devices: 83.7 us -> none  [shards(): cotangent_all = lax.all_gather(expected_cot, 'markov', axis=0, tiled=True)]
    ppermute x0 -> x3, waiting for transfers between devices: none -> 66.3 us  [the longest x2 45.5 us: shards(): x_next = jax.lax.ppermute(x_next, 'markov', arrivals)]
    all_gather x1, waiting for transfers between devices: 24.5 us -> 0.01 us  [shards(): lax.all_gather(transition, ('storage', 'sub'), axis=0, tiled=True)]
    all_to_all x1, waiting for transfers between devices: 75.7 us -> 60.2 us  [shards(): lax.all_to_all(cotangent_all, ('storage', 'sub'), split_axis=0, concat_ax...]
    ppermute x0 -> x3, starting transfers between devices: none -> 5.2 us  [the longest x2 3.11 us: shards(): x_next = jax.lax.ppermute(x_next, 'markov', arrivals)]
    unnamed x0 -> x5, local copies, waits for them, and re-layouts: none -> 3.73 us
  transfers between devices with their start and end apart: 4 -> 6, of which waited for: 3 -> 4; matrix products, arithmetic and copies ran while one was open for 7% -> 10% of each run, Pallas kernels for 0% -> 0%
where the time goes in v1:
time: 183 us
  waiting for transfers between devices  128 us (70%)
  matrix products  18.2 us (10%)
  between operations  14.8 us (8%)
  local copies, waits for them, and re-layouts  12.1 us (7%)
  starting transfers between devices  10.1 us (6%)
    all_to_all x1, waiting for transfers between devices, shards(): lax.all_to_all(cotangent_all, ('storage', 'sub'), split_axis=0, concat_ax...  60.2 us
    ppermute x2, waiting for transfers between devices, shards(): x_next = jax.lax.ppermute(x_next, 'markov', arrivals)  45.5 us
    ppermute x1, waiting for transfers between devices, shards(): q_next = jax.lax.ppermute(q_next, 'markov', bank)  20.8 us
    dot_general x1, matrix products, shards(): lax.dot_general(own_states, gathered_values, (((1,), (1,)), ((), ())), pr...  10 us
    dot_general x1, matrix products, shards(): lax.dot_general(lax.all_gather(transition, ('storage', 'sub'), axis=0, ti...  8.22 us
    all_to_all x1, local copies, waits for them, and re-layouts, shards(): lax.all_to_all(cotangent_all, ('storage', 'sub'), split_axis=0, concat_ax...  6.35 us
    all_to_all x1, starting transfers between devices, shards(): lax.all_to_all(cotangent_all, ('storage', 'sub'), split_axis=0, concat_ax...  4.83 us
    unnamed x5, local copies, waits for them, and re-layouts  3.73 us
  transfers between devices with their start and end apart: 6, of which 4 were waited for; matrix products, arithmetic and copies ran while one was open for 10% of the time, Pallas kernels for 0%

profile of v1, /device:TPU:0, one launch (start us, length us, event | category | flops | bytes accessed | tf_op | source)
XLA Modules:
  0.0 183.1 jit_solution(16305576197843233352)
XLA Ops:
  7.2 0.0 copy-start.1
  7.2 0.0 all-gather.5.cloned.1.call-start
  7.2 0.7 all-gather.5.cloned.1.call-update
  7.9 0.0 all-gather.3.cloned.1.call-start
  8.0 0.7 all-gather.3.cloned.1.call-update
  8.7 3.1 %collective-permute-start = (bf16[1024,512]{1,0:T(8,128)(2,1)}, bf16[1024,512]{1,0:T(8,128)(2,1)S(1)}, u32[]{:S(2)}, u32[]{:S(2)}) collective-permute-start(bf16[1024,512]{1,0:T(8,128)(2,1)} %param.4), channel_id=1, source_target_pairs={{0,4},{4,8},{8,12},{12,0},{1,5},{5,9},{9,13},{13,1},{2,6},{6,10},{... | collective-permute-start | bytes 3145736 | tf_op jit(solution)/shard_map/ppermute | solution.py:24
  11.8 2.1 %collective-permute-start.1 = (bf16[1024,512]{1,0:T(8,128)(2,1)}, bf16[1024,512]{1,0:T(8,128)(2,1)}, u32[]{:S(2)}, u32[]{:S(2)}) collective-permute-start(bf16[1024,512]{1,0:T(8,128)(2,1)} %param.4), channel_id=1, source_target_pairs={{0,12},{4,0},{8,4},{12,8},{1,13},{5,1},{9,5},{13,9},{2,14},{6,2},{... | collective-permute-start | bytes 3145736 | tf_op jit(solution)/shard_map/ppermute | solution.py:32
  13.9 24.2 %collective-permute-done = bf16[1024,512]{1,0:T(8,128)(2,1)S(1)} collective-permute-done((bf16[1024,512]{1,0:T(8,128)(2,1)}, bf16[1024,512]{1,0:T(8,128)(2,1)S(1)}, u32[]{:S(2)}, u32[]{:S(2)}) %collective-permute-start) | collective-permute-done | bytes 1048608 | tf_op jit(solution)/shard_map/ppermute | solution.py:24
  38.1 0.0 collective-permute-start.2
  38.1 0.3 broadcast_in_dim.3
  38.3 0.0 copy-done.1
  38.3 0.1 constant_dynamic-update-slice_fusion.3
  38.5 0.1 constant_dynamic-update-slice_fusion.2
  38.6 20.8 %collective-permute-done.1 = bf16[1024,512]{1,0:T(8,128)(2,1)} collective-permute-done((bf16[1024,512]{1,0:T(8,128)(2,1)}, bf16[1024,512]{1,0:T(8,128)(2,1)}, u32[]{:S(2)}, u32[]{:S(2)}) %collective-permute-start.1) | collective-permute-done | bytes 1048608 | tf_op jit(solution)/shard_map/ppermute | solution.py:32
  59.4 1.4 constant_dynamic-update-slice_fusion.1
  60.8 21.3 %collective-permute-done.2 = bf16[1024,512]{1,0:T(8,128)(2,1)S(1)} collective-permute-done((bf16[1024,512]{1,0:T(8,128)(2,1)S(1)}, bf16[1024,512]{1,0:T(8,128)(2,1)S(1)}, u32[]{:S(2)}, u32[]{:S(2)}) %collective-permute-start.2) | collective-permute-done | bytes 1048608 | tf_op jit(solution)/shard_map/ppermute | solution.py:24
  82.1 0.1 constant_dynamic-update-slice_fusion
  82.2 0.0 copy-start
  82.3 1.9 %copy-done = bf16[4096,512]{1,0:T(8,128)(2,1)} copy-done((bf16[4096,512]{1,0:T(8,128)(2,1)}, bf16[4096,512]{1,0:T(8,128)(2,1)S(1)}, u32[]{:S(2)}) %copy-start) | copy-done | bytes 4194328
  84.2 4.8 %all-to-all-start = ((bf16[4,1024,512]{2,1,0:T(8,128)(2,1)}), bf16[4,1024,512]{2,1,0:T(8,128)(2,1)}, u32[]{:S(2)}, u32[]{:S(2)}) async-start(bf16[4,1024,512]{2,1,0:T(8,128)(2,1)} %bitcast.10), calls=%async_computation | async-start | bytes 8388608 | tf_op jit(solution)/shard_map/all_to_all | solution.py:42
  89.7 60.2 %all-to-all-done = bf16[4,1024,512]{2,1,0:T(8,128)(2,1)} async-done(((bf16[4,1024,512]{2,1,0:T(8,128)(2,1)}), bf16[4,1024,512]{2,1,0:T(8,128)(2,1)}, u32[]{:S(2)}, u32[]{:S(2)}) %all-to-all-start) | async-done | bytes 4194336 | tf_op jit(solution)/shard_map/all_to_all | solution.py:42
  149.9 6.4 %copy.8 = bf16[1024,4,512]{0,2,1:T(8,128)(2,1)} copy(bf16[1024,4,512]{2,0,1:T(8,128)(2,1)} %bitcast.3) | data formatting | bytes 8388608 | tf_op jit(solution)/shard_map/all_to_all | solution.py:42
  156.2 0.0 all-gather.5.cloned.1.call-done
  156.2 10.0 %convolution_multiply_fusion = f32[1024,1024]{1,0:T(8,128)} fusion(bf16[1024,2048]{0,1:T(8,128)(2,1)} %bitcast.11, bf16[1024,2048]{1,0:T(8,128)(2,1)} %all-gather.5.cloned.1.call-done, f32[]{:T(128)} %bitcast), kind=kOutput, calls=%fused_computation | convolution fusion | flops 4296015872 | bytes 12582916 | tf_op jit(solution)/shard_map/dot_general | solution.py:46
  166.2 0.0 all-gather.3.cloned.1.call-done
  166.2 8.2 %multiply_bitcast_fusion = f32[1024,512]{0,1:T(8,128)S(1)} fusion(bf16[4096,512]{1,0:T(8,128)(2,1)} %copy-done, bf16[4096,1024]{1,0:T(8,128)(2,1)} %all-gather.3.cloned.1.call-done, f32[]{:T(128)} %bitcast), kind=kOutput, calls=%fused_computation.1 | convolution fusion | flops 4295491584 | bytes 14680068 | tf_op jit(solution)/shard_map/dot_general | solution.py:36
  174.5 1.8 copy.9
Async XLA Ops:
  7.2 31.2 %copy-start.1 = (bf16[1024,512]{1,0:T(8,128)(2,1)S(1)}, bf16[1024,512]{1,0:T(8,128)(2,1)}, u32[]{:S(2)}) copy-start(bf16[1024,512]{1,0:T(8,128)(2,1)} %param.4) | copy-start | bytes 3145732
  7.2 149.0 %all-gather.5.cloned.1.call-start = ((), (), s32[]{:S(2)}) async-start(), calls=%async_computation.2 | async-start | bytes 5242880 | tf_op jit(solution)/shard_map/all_gather | solution.py:45
  7.9 158.3 %all-gather.3.cloned.1.call-start = ((), (), s32[]{:S(2)}) async-start(), calls=%async_computation.1 | async-start | bytes 10485760 | tf_op jit(solution)/shard_map/all_gather | solution.py:37
  8.7 29.4 %collective-permute-start = (bf16[1024,512]{1,0:T(8,128)(2,1)}, bf16[1024,512]{1,0:T(8,128)(2,1)S(1)}, u32[]{:S(2)}, u32[]{:S(2)}) collective-permute-start(bf16[1024,512]{1,0:T(8,128)(2,1)} %param.4), channel_id=1, source_target_pairs={{0,4},{4,8},{8,12},{12,0},{1,5},{5,9},{9,13},{13,1},{2,6},{6,10},{... | collective-permute-start | bytes 3145736 | tf_op jit(solution)/shard_map/ppermute | solution.py:24
  11.8 47.6 %collective-permute-start.1 = (bf16[1024,512]{1,0:T(8,128)(2,1)}, bf16[1024,512]{1,0:T(8,128)(2,1)}, u32[]{:S(2)}, u32[]{:S(2)}) collective-permute-start(bf16[1024,512]{1,0:T(8,128)(2,1)} %param.4), channel_id=1, source_target_pairs={{0,12},{4,0},{8,4},{12,8},{1,13},{5,1},{9,5},{13,9},{2,14},{6,2},{... | collective-permute-start | bytes 3145736 | tf_op jit(solution)/shard_map/ppermute | solution.py:32
  38.1 44.1 %collective-permute-start.2 = (bf16[1024,512]{1,0:T(8,128)(2,1)S(1)}, bf16[1024,512]{1,0:T(8,128)(2,1)S(1)}, u32[]{:S(2)}, u32[]{:S(2)}) collective-permute-start(bf16[1024,512]{1,0:T(8,128)(2,1)S(1)} %collective-permute-done), channel_id=1, source_target_pairs={{0,4},{4,8},{8,12},{12,0},{1,5},{5,9},{9,13},{13,1},{2,6},{6,10},{... | collective-permute-start | bytes 3145736 | tf_op jit(solution)/shard_map/ppermute | solution.py:24
  82.2 1.9 %copy-start = (bf16[4096,512]{1,0:T(8,128)(2,1)}, bf16[4096,512]{1,0:T(8,128)(2,1)S(1)}, u32[]{:S(2)}) copy-start(bf16[4096,512]{1,0:T(8,128)(2,1)S(1)} %constant_dynamic-update-slice_fusion) | copy-start | bytes 12582916
  84.2 65.7 %all-to-all-start = ((bf16[4,1024,512]{2,1,0:T(8,128)(2,1)}), bf16[4,1024,512]{2,1,0:T(8,128)(2,1)}, u32[]{:S(2)}, u32[]{:S(2)}) async-start(bf16[4,1024,512]{2,1,0:T(8,128)(2,1)} %bitcast.10), calls=%async_computation | async-start | bytes 8388608 | tf_op jit(solution)/shard_map/all_to_all | solution.py:42
Sparse Core Ops, SparseCore 0:
  9.5 37.1 all-gather.4
  48.3 70.9 all-gather.2

commit v2 on v0

--- a/solution.py
+++ b/solution.py
@@ -6,11 +6,18 @@
 discount_rate = 0.97
 
 
+def exchange_gather(value, axis, dim):
+    peers = lax.axis_size(axis)
+    shards = jnp.stack([value for _ in range(peers)])
+    shards = lax.all_to_all(shards, axis, split_axis=0, concat_axis=0)
+    return jnp.concatenate(shards, axis=dim)
+
+
 def shards(expected_cot, value_next, transition, section):
     discount_factor = jnp.exp(section[0].astype(jnp.float32) * jnp.log(jnp.float32(discount_rate)))
     cotangent_all = lax.all_gather(expected_cot, "markov", axis=0, tiled=True)
     adjoint_sum = lax.dot_general(
-        lax.all_gather(transition, ("storage", "sub"), axis=0, tiled=True),
+        exchange_gather(transition, ("storage", "sub"), 0),
         cotangent_all,
         (((0,), (0,)), ((), ())),
         preferred_element_type=jnp.float32,

time: 232 us -> 204 us (0.88)
  waiting for transfers between devices: 186 us -> 146 us
  local copies, waits for them, and re-layouts: 6.35 us -> 12.3 us
  starting transfers between devices: 4.97 us -> 10.6 us
    all_to_all x0 -> x1, waiting for transfers between devices: none -> 104 us  [exchange_gather(): shards = lax.all_to_all(shards, axis, split_axis=0, concat_axis=0)]
    all_gather x1, waiting for transfers between devices: 83.7 us -> 0.01 us  [shards(): cotangent_all = lax.all_gather(expected_cot, 'markov', axis=0, tiled=True)]
    all_to_all x1, waiting for transfers between devices: 75.7 us -> 40.8 us  [shards(): lax.all_to_all(cotangent_all, ('storage', 'sub'), split_axis=0, concat_ax...]
    all_gather x1 -> x0, waiting for transfers between devices: 24.5 us -> none  [shards(): lax.all_gather(transition, ('storage', 'sub'), axis=0, tiled=True)]
    another operation x0 -> x1, local copies, waits for them, and re-layouts: none -> 6.02 us  [exchange_gather(): shards = jnp.stack([value for _ in range(peers)])]
    all_to_all x0 -> x1, starting transfers between devices: none -> 5.64 us  [exchange_gather(): shards = lax.all_to_all(shards, axis, split_axis=0, concat_axis=0)]
  transfers between devices with their start and end apart: 4 -> 4, of which waited for: 3 -> 2; matrix products, arithmetic and copies ran while one was open for 7% -> 11% of each run, Pallas kernels for 0% -> 0%
where the time goes in v2:
time: 204 us
  waiting for transfers between devices  146 us (72%)
  matrix products  20.5 us (10%)
  between operations  14.7 us (7%)
  local copies, waits for them, and re-layouts  12.3 us (6%)
  starting transfers between devices  10.6 us (5%)
    all_to_all x1, waiting for transfers between devices, exchange_gather(): shards = lax.all_to_all(shards, axis, split_axis=0, concat_axis=0)  104 us
    all_to_all x1, waiting for transfers between devices, shards(): lax.all_to_all(cotangent_all, ('storage', 'sub'), split_axis=0, concat_ax...  40.8 us
    dot_general x1, matrix products, shards(): lax.dot_general(exchange_gather(transition, ('storage', 'sub'), 0), cotan...  10.5 us
    dot_general x1, matrix products, shards(): lax.dot_general(own_states, gathered_values, (((1,), (1,)), ((), ())), pr...  10 us
    all_to_all x1, local copies, waits for them, and re-layouts, shards(): lax.all_to_all(cotangent_all, ('storage', 'sub'), split_axis=0, concat_ax...  6.3 us
    another operation x1, local copies, waits for them, and re-layouts, exchange_gather(): shards = jnp.stack([value for _ in range(peers)])  6.02 us
    all_to_all x1, starting transfers between devices, exchange_gather(): shards = lax.all_to_all(shards, axis, split_axis=0, concat_axis=0)  5.64 us
    all_to_all x1, starting transfers between devices, shards(): lax.all_to_all(cotangent_all, ('storage', 'sub'), split_axis=0, concat_ax...  4.92 us
  transfers between devices with their start and end apart: 4, of which 2 were waited for; matrix products, arithmetic and copies ran while one was open for 11% of the time, Pallas kernels for 0%

profile of v2, /device:TPU:0, one launch (start us, length us, event | category | flops | bytes accessed | tf_op | source)
XLA Modules:
  0.0 204.0 jit_solution(6479692169010101072)
XLA Ops:
  7.2 0.0 all-gather.3.cloned.1.call-start
  7.2 0.7 all-gather.3.cloned.1.call-update
  7.9 6.0 %stack.2 = bf16[4,1024,1024]{2,1,0:T(8,128)(2,1)} broadcast(bf16[1024,1024]{1,0:T(8,128)(2,1)} %param.6), dimensions={1,2} | broadcast | bytes 10485760 | tf_op jit(solution)/shard_map/stack | solution.py:11
  13.9 5.6 %all-to-all-start = ((bf16[4,1024,1024]{2,1,0:T(8,128)(2,1)}), bf16[4,1024,1024]{2,1,0:T(8,128)(2,1)}, u32[]{:S(2)}, u32[]{:S(2)}) async-start(bf16[4,1024,1024]{2,1,0:T(8,128)(2,1)} %stack.2), calls=%async_computation | async-start | bytes 16777216 | tf_op jit(solution)/shard_map/all_to_all | solution.py:12
  19.6 0.0 all-gather.5.cloned.1.call-start
  19.6 0.7 all-gather.5.cloned.1.call-update
  20.3 103.6 %all-to-all-done = bf16[4,1024,1024]{2,1,0:T(8,128)(2,1)} async-done(((bf16[4,1024,1024]{2,1,0:T(8,128)(2,1)}), bf16[4,1024,1024]{2,1,0:T(8,128)(2,1)}, u32[]{:S(2)}, u32[]{:S(2)}) %all-to-all-start) | async-done | bytes 8388640 | tf_op jit(solution)/shard_map/all_to_all | solution.py:12
  124.0 0.0 all-gather.3.cloned.1.call-done
  124.0 4.9 %all-to-all-start.1 = ((bf16[4,1024,512]{2,1,0:T(8,128)(2,1)}), bf16[4,1024,512]{2,1,0:T(8,128)(2,1)}, u32[]{:S(2)}, u32[]{:S(2)}) async-start(bf16[4,1024,512]{2,1,0:T(8,128)(2,1)} %bitcast.9), calls=%async_computation.1 | async-start | bytes 8388608 | tf_op jit(solution)/shard_map/all_to_all | solution.py:25
  129.6 10.5 %convolution_multiply_fusion.1 = f32[1024,512]{1,0:T(8,128)} fusion(bf16[4096,1024]{1,0:T(8,128)(2,1)} %bitcast.1, bf16[4096,512]{1,0:T(8,128)(2,1)} %all-gather.3.cloned.1.call-done, f32[]{:T(128)} %bitcast), kind=kOutput, calls=%fused_computation.1 | convolution fusion | flops 4295491584 | bytes 14680068 | tf_op jit(solution)/shard_map/dot_general | solution.py:19
  140.0 40.8 %all-to-all-done.1 = bf16[4,1024,512]{2,1,0:T(8,128)(2,1)} async-done(((bf16[4,1024,512]{2,1,0:T(8,128)(2,1)}), bf16[4,1024,512]{2,1,0:T(8,128)(2,1)}, u32[]{:S(2)}, u32[]{:S(2)}) %all-to-all-start.1) | async-done | bytes 4194336 | tf_op jit(solution)/shard_map/all_to_all | solution.py:25
  180.8 6.3 %copy.6 = bf16[1024,4,512]{0,2,1:T(8,128)(2,1)} copy(bf16[1024,4,512]{2,0,1:T(8,128)(2,1)} %bitcast.3) | data formatting | bytes 8388608 | tf_op jit(solution)/shard_map/all_to_all | solution.py:25
  187.1 0.0 all-gather.5.cloned.1.call-done
  187.1 10.0 %convolution_multiply_fusion = f32[1024,1024]{1,0:T(8,128)} fusion(bf16[1024,2048]{0,1:T(8,128)(2,1)} %bitcast.10, bf16[1024,2048]{1,0:T(8,128)(2,1)} %all-gather.5.cloned.1.call-done, f32[]{:T(128)} %bitcast), kind=kOutput, calls=%fused_computation | convolution fusion | flops 4296015872 | bytes 12582916 | tf_op jit(solution)/shard_map/dot_general | solution.py:29
Async XLA Ops:
  7.2 116.8 %all-gather.3.cloned.1.call-start = ((), (), s32[]{:S(2)}) async-start(), calls=%async_computation.2 | async-start | bytes 5242880 | tf_op jit(solution)/shard_map/all_gather | solution.py:18
  13.9 110.0 %all-to-all-start = ((bf16[4,1024,1024]{2,1,0:T(8,128)(2,1)}), bf16[4,1024,1024]{2,1,0:T(8,128)(2,1)}, u32[]{:S(2)}, u32[]{:S(2)}) async-start(bf16[4,1024,1024]{2,1,0:T(8,128)(2,1)} %stack.2), calls=%async_computation | async-start | bytes 16777216 | tf_op jit(solution)/shard_map/all_to_all | solution.py:12
  19.6 167.5 %all-gather.5.cloned.1.call-start = ((), (), s32[]{:S(2)}) async-start(), calls=%async_computation.3 | async-start | bytes 5242880 | tf_op jit(solution)/shard_map/all_gather | solution.py:28
  124.0 56.8 %all-to-all-start.1 = ((bf16[4,1024,512]{2,1,0:T(8,128)(2,1)}), bf16[4,1024,512]{2,1,0:T(8,128)(2,1)}, u32[]{:S(2)}, u32[]{:S(2)}) async-start(bf16[4,1024,512]{2,1,0:T(8,128)(2,1)} %bitcast.9), calls=%async_computation.1 | async-start | bytes 8388608 | tf_op jit(solution)/shard_map/all_to_all | solution.py:25
Sparse Core Ops, SparseCore 0:
  9.5 83.4 all-gather.2
  94.6 46.1 all-gather.4
